TPU v7x, 32 devices: a whole 2x2x4 slice. The times are simulated.
32 devices in a mesh: gx: 8 (over y, x, core), gy: 4 (over z).
Axes of the slice: x: 2, y: 2, z: 4, core: 2. Of those that a mesh axis runs over, the one named last changes fastest.
Arguments:
- right_side: float32 [2, 128, 512], P(None, 'gx', 'gy'), may hold values from -160 to 160
- conductivity: float32 [128, 512], P('gx', 'gy'), may hold values from 0.2 to 5
- leaf_inverse: float32 [32, 16, 128, 128], P('gx', 'gy'), may hold values from -1 to 4, as said below
- front_basis: float32 [128, 512, 128], P('gx', 'gy'), may hold values from -0.25 to 0.25
- leaf_transfer: float32 [8, 4, 128, 128], P('gx', 'gy'), may hold values from -0.4375 to 0.4375
- node_transfer: float32 [8, 4, 4, 128, 128], P('gx', 'gy'), may hold values from -1 to 1, as said below
- leaf_front: float32 [8, 4, 128, 128], P('gx', 'gy'), may hold values from -1 to 1, as said below
- node_front: float32 [8, 4, 5, 128, 128], P('gx', 'gy'), may hold values from -1 to 1, as said below
Outputs:
- solution: float32 [2, 128, 512], P(None, 'gx', 'gy')
- residual: float32 [2, 128, 512], P(None, 'gx', 'gy')
- direction: float32 [2, 128, 512], P(None, 'gx', 'gy')
Inputs may be any that keep to these rules, and one draw needn't show every extreme that they name: `leaf_inverse`: every block is symmetric and positive definite. `leaf_front`: every matrix is symmetric and positive definite. `node_front`: every matrix is symmetric and positive definite; entry h - 1 is the same for all tiles covered by one node of level h. `node_transfer`: entry h - 1 is the same for all tiles covered by one node of level h.
All inputs are finite; a program needn't handle non-finite values.
Results may differ from a plain program's by a relative error of at most 0.0001.
Values sent between devices are 32-bit elements; how exact they have to be, the bound alone decides.
No kernel may reach another device: no remote copies, remote signals or barrier semaphores. Data moves between devices by JAX's collectives and lax.ppermute only.
A program may use at most 64 MiB of HBM per device.

v0:
```python
from functools import partial
import jax
import jax.numpy as jnp
from jax import lax
from jax.sharding import PartitionSpec as P

LBX = 4
LBY = 32
HIGHEST = lax.Precision.HIGHEST


def extended(cells, sides, width):
    for axis, dim in sides:
        count = lax.axis_size(axis)
        ends = count - 1
        head = lax.slice_in_dim(cells, 0, width, axis=dim)
        tail = lax.slice_in_dim(cells, cells.shape[dim] - width, cells.shape[dim], axis=dim)
        cells = jnp.concatenate(
            [
                lax.ppermute(tail, axis, [(i, (i + 1) % count) for i in range(ends)]),
                cells,
                lax.ppermute(head, axis, [((i + 1) % count, i) for i in range(ends)]),
            ],
            axis=dim,
        )
    return cells


def from_partner(value, axis, distance):
    mask = 2**distance
    pairs = [(source, source ^ mask) for source in range(lax.axis_size(axis))]
    return lax.ppermute(value, axis, pairs)


def operate_padded(padded, padded_k):
    extent_x = padded.shape[1] - 2
    extent_y = padded.shape[2] - 2
    center = padded[:, 1:-1, 1:-1]
    center_k = padded_k[1:-1, 1:-1]
    summed = jnp.zeros_like(center)
    for offset_x, offset_y in ((2, 1), (0, 1), (1, 2), (1, 0)):
        beside = padded[:, offset_x : offset_x + extent_x, offset_y : offset_y + extent_y]
        beside_k = padded_k[offset_x : offset_x + extent_x, offset_y : offset_y + extent_y]
        summed = summed + 0.5 * (center_k + beside_k) * (center - beside)
    return summed


def stencil(values, conductivity):
    stacked = jnp.concatenate([values, conductivity[None]], axis=0)
    padded = extended(stacked, (("gx", 1), ("gy", 2)), 1)
    return operate_padded(padded[:-1], padded[-1])


def leaf_apply(values, leaf_inverse):
    count_s, extent_x, extent_y = values.shape
    blocks_x = extent_x // LBX
    blocks_y = extent_y // LBY
    grouped = values.reshape(count_s, blocks_x, LBX, blocks_y, LBY).transpose(0, 1, 3, 2, 4)
    grouped = grouped.reshape(count_s, blocks_x, blocks_y, LBX * LBY)
    mapped = jnp.einsum("xyij,sxyj->sxyi", leaf_inverse, grouped, precision=HIGHEST)
    mapped = mapped.reshape(count_s, blocks_x, blocks_y, LBX, LBY).transpose(0, 1, 3, 2, 4)
    return mapped.reshape(count_s, extent_x, extent_y)


def spread_tree(coeffs, leaf_transfer, node_transfer, leaf_front, node_front):
    levels = lax.axis_size(("gx", "gy")).bit_length() - 1
    leaf_t = leaf_transfer[0, 0]
    leaf_f = leaf_front[0, 0]
    node_t = node_transfer[0, 0]
    node_f = node_front[0, 0]
    uppers = [coeffs]
    moving = jnp.dot(coeffs, leaf_t, precision=HIGHEST)
    for height in range(1, levels + 1):
        partner = from_partner(moving, ("gx", "gy"), height - 1)
        summed = moving + partner
        uppers.append(summed)
        if height < levels:
            moving = jnp.dot(summed, node_t[height - 1], precision=HIGHEST)
    downward = jnp.dot(uppers[levels], node_f[levels - 1], precision=HIGHEST)
    for height in range(levels, 1, -1):
        downward = jnp.dot(downward, node_t[height - 2].T, precision=HIGHEST) + jnp.dot(
            uppers[height - 1], node_f[height - 2], precision=HIGHEST
        )
    return jnp.dot(downward, leaf_t.T, precision=HIGHEST) + jnp.dot(
        coeffs, leaf_f, precision=HIGHEST
    )


def precondition(
    values, leaf_inverse, front_basis, leaf_transfer, node_transfer, leaf_front, node_front
):
    near = leaf_apply(values, leaf_inverse)
    coeffs = jnp.einsum("sab,abk->sk", values, front_basis, precision=HIGHEST)
    spread = spread_tree(coeffs, leaf_transfer, node_transfer, leaf_front, node_front)
    return near + jnp.einsum("sk,abk->sab", spread, front_basis, precision=HIGHEST)


def on_device(
    right_side,
    conductivity,
    leaf_inverse,
    front_basis,
    leaf_transfer,
    node_transfer,
    leaf_front,
    node_front,
):
    apply_inverse = partial(
        precondition,
        leaf_inverse=leaf_inverse,
        front_basis=front_basis,
        leaf_transfer=leaf_transfer,
        node_transfer=node_transfer,
        leaf_front=leaf_front,
        node_front=node_front,
    )
    first_z = apply_inverse(right_side)
    local_rz = jnp.sum(right_side * first_z, axis=(1, 2))
    rz_old = lax.psum(local_rz, ("gx", "gy"))
    applied = stencil(first_z, conductivity)
    curvature = lax.psum(jnp.sum(first_z * applied, axis=(1, 2)), ("gx", "gy"))
    step_size = (rz_old / curvature)[:, None, None]
    solution = step_size * first_z
    residual = right_side - step_size * applied
    second_z = first_z - step_size * apply_inverse(applied)
    rz_new = lax.psum(jnp.sum(residual * second_z, axis=(1, 2)), ("gx", "gy"))
    direction = second_z + (rz_new / rz_old)[:, None, None] * first_z
    return (solution, residual, direction)


def solution(mesh):
    return jax.shard_map(
        on_device,
        mesh=mesh,
        in_specs=(
            P(None, "gx", "gy"),
            P("gx", "gy"),
            P("gx", "gy", None, None),
            P("gx", "gy", None),
            P("gx", "gy", None, None),
            P("gx", "gy", None, None, None),
            P("gx", "gy", None, None),
            P("gx", "gy", None, None, None),
        ),
        out_specs=(P(None, "gx", "gy"), P(None, "gx", "gy"), P(None, "gx", "gy")),
        check_vma=False,
    )
```

profile of v0, /device:TPU:0, one launch (start us, length us, event | category | flops | bytes accessed | tf_op | source)
XLA Modules:
  0.0 145.0 jit_solution(14396985049537503632)
XLA Ops:
  0.7 1.2 copy-done
  1.9 1.3 convolution_bitcast_fusion.3
  3.4 3.1 %collective-permute-start = (f32[2,128]{1,0:T(2,128)S(1)}, f32[2,128]{1,0:T(2,128)S(1)}, u32[]{:S(2)}, u32[]{:S(2)}) collective-permute-start(f32[2,128]{1,0:T(2,128)S(1)} %fusion.56), channel_id=1, source_target_pairs={{0,1},{1,0},{2,3},{3,2},{4,5},{5,4},{6,7},{7,6},{8,9},{9,8},{10,11... | collective-permute-start | bytes 3080 | tf_op jit(solution)/shard_map/ppermute | solution.py:32
  6.4 1.6 %collective-permute-done = f32[2,128]{1,0:T(2,128)S(1)} collective-permute-done((f32[2,128]{1,0:T(2,128)S(1)}, f32[2,128]{1,0:T(2,128)S(1)}, u32[]{:S(2)}, u32[]{:S(2)}) %collective-permute-start) | collective-permute-done | bytes 1056 | tf_op jit(solution)/shard_map/ppermute | solution.py:32
  8.1 3.1 %collective-permute-start.1 = (f32[2,128]{1,0:T(2,128)S(1)}, f32[2,128]{1,0:T(2,128)S(1)}, u32[]{:S(2)}, u32[]{:S(2)}) collective-permute-start(f32[2,128]{1,0:T(2,128)S(1)} %fusion.48), channel_id=1, source_target_pairs={{0,2},{1,3},{2,0},{3,1},{4,6},{5,7},{6,4},{7,5},{8,10},{9,11},{10,... | collective-permute-start | bytes 3080 | tf_op jit(solution)/shard_map/ppermute | solution.py:32
  11.2 1.6 %collective-permute-done.1 = f32[2,128]{1,0:T(2,128)S(1)} collective-permute-done((f32[2,128]{1,0:T(2,128)S(1)}, f32[2,128]{1,0:T(2,128)S(1)}, u32[]{:S(2)}, u32[]{:S(2)}) %collective-permute-start.1) | collective-permute-done | bytes 1056 | tf_op jit(solution)/shard_map/ppermute | solution.py:32
  12.9 1.2 collective-permute-done.2
  14.2 1.8 %collective-permute-start.3 = (f32[2,128]{1,0:T(2,128)S(1)}, f32[2,128]{1,0:T(2,128)S(1)}, u32[]{:S(2)}, u32[]{:S(2)}) collective-permute-start(f32[2,128]{1,0:T(2,128)S(1)} %fusion.32), channel_id=1, source_target_pairs={{0,8},{1,9},{2,10},{3,11},{4,12},{5,13},{6,14},{7,15},{8,0},{9,1},... | collective-permute-start | bytes 3080 | tf_op jit(solution)/shard_map/ppermute | solution.py:32
  16.1 0.8 reshape.54
  17.0 0.8 collective-permute-done.3
  18.0 1.9 %collective-permute-start.4 = (f32[2,128]{1,0:T(2,128)S(1)}, f32[2,128]{1,0:T(2,128)S(1)}, u32[]{:S(2)}, u32[]{:S(2)}) collective-permute-start(f32[2,128]{1,0:T(2,128)S(1)} %fusion.24), channel_id=1, source_target_pairs={{0,16},{1,17},{2,18},{3,19},{4,20},{5,21},{6,22},{7,23},{8,24},{9,... | collective-permute-start | bytes 3080 | tf_op jit(solution)/shard_map/ppermute | solution.py:32
  19.9 1.7 %convolution_bitcast_fusion.1 = f32[2,4,4,128]{3,0,2,1:T(2,128)S(1)} fusion(f32[2,4,4,128]{3,0,2,1:T(2,128)S(1)} %reshape.55, f32[4,4,128,128]{3,2,1,0:T(8,128)S(1)} %copy-done.2), kind=kOutput, calls=%fused_computation.1 | convolution fusion | flops 6291456 | bytes 1081344 | tf_op jit(solution)/shard_map/xyij,sxyj->sxyi/dot_general | solution.py:60
  22.2 0.2 convolution_add_fusion.11
  22.6 0.2 convolution_add_fusion.10
  23.0 0.2 convolution_add_fusion.9
  23.4 0.2 convolution_add_fusion.8
  23.8 0.5 copy-done.6
  24.4 1.0 convolution_add_fusion.1
  25.4 1.3 collective-permute-start.6
  26.7 3.0 %collective-permute-start.5 = (f32[3,1,128]{2,0,1:T(4,128)S(1)}, f32[3,1,128]{2,0,1:T(4,128)S(1)}, u32[]{:S(2)}, u32[]{:S(2)}) collective-permute-start(f32[3,1,128]{2,0,1:T(4,128)S(1)} %get-tuple-element.19), channel_id=1, source_target_pairs={{0,4},{4,8},{8,12},{12,16},{16,20},{20,24},{24,28},{1,5},{5,9},{9,... | collective-permute-start | bytes 4616 | tf_op jit(solution)/shard_map/ppermute | solution.py:20
  29.8 0.8 collective-permute-done.5
  30.7 3.5 %collective-permute-start.7 = (f32[3,18,1]{2,0,1:T(4,128)S(1)}, f32[3,18,1]{2,0,1:T(4,128)S(1)}, u32[]{:S(2)}, u32[]{:S(2)}) collective-permute-start(f32[3,18,1]{2,0,1:T(4,128)S(1)} %get-tuple-element.14), channel_id=1, source_target_pairs={{0,1},{1,2},{2,3},{4,5},{5,6},{6,7},{8,9},{9,10},{10,11},{12,13},{... | collective-permute-start | bytes 656 | tf_op jit(solution)/shard_map/ppermute | solution.py:20
  34.2 1.3 collective-permute-start.8
  35.5 0.5 collective-permute-done.7
  36.0 4.2 %collective-permute-done.8 = f32[3,18,1]{2,0,1:T(4,128)S(1)} collective-permute-done((f32[3,18,1]{2,0,1:T(4,128)S(1)}, f32[3,18,1]{2,0,1:T(4,128)S(1)}, u32[]{:S(2)}, u32[]{:S(2)}) %collective-permute-start.8) | collective-permute-done | bytes 248 | tf_op jit(solution)/shard_map/ppermute | solution.py:22
  40.5 0.6 copy-done.5
  41.1 0.3 multiply_reduce_fusion.1
  41.4 0.6 convolution_bitcast_fusion.2
  42.2 1.6 %collective-permute-start.9 = (f32[2,128]{1,0:T(2,128)S(1)}, f32[2,128]{1,0:T(2,128)S(1)}, u32[]{:S(2)}, u32[]{:S(2)}) collective-permute-start(f32[2,128]{1,0:T(2,128)S(1)} %fusion.52), channel_id=1, source_target_pairs={{0,1},{1,0},{2,3},{3,2},{4,5},{5,4},{6,7},{7,6},{8,9},{9,8},{10,11... | collective-permute-start | bytes 3080 | tf_op jit(solution)/shard_map/ppermute | solution.py:32
  43.8 2.0 %collective-permute-done.9 = f32[2,128]{1,0:T(2,128)S(1)} collective-permute-done((f32[2,128]{1,0:T(2,128)S(1)}, f32[2,128]{1,0:T(2,128)S(1)}, u32[]{:S(2)}, u32[]{:S(2)}) %collective-permute-start.9) | collective-permute-done | bytes 1056 | tf_op jit(solution)/shard_map/ppermute | solution.py:32
  45.9 2.6 %collective-permute-start.10 = (f32[2,128]{1,0:T(2,128)S(1)}, f32[2,128]{1,0:T(2,128)S(1)}, u32[]{:S(2)}, u32[]{:S(2)}) collective-permute-start(f32[2,128]{1,0:T(2,128)S(1)} %fusion.44), channel_id=1, source_target_pairs={{0,2},{1,3},{2,0},{3,1},{4,6},{5,7},{6,4},{7,5},{8,10},{9,11},{10,... | collective-permute-start | bytes 3080 | tf_op jit(solution)/shard_map/ppermute | solution.py:32
  48.5 1.9 %collective-permute-done.10 = f32[2,128]{1,0:T(2,128)S(1)} collective-permute-done((f32[2,128]{1,0:T(2,128)S(1)}, f32[2,128]{1,0:T(2,128)S(1)}, u32[]{:S(2)}, u32[]{:S(2)}) %collective-permute-start.10) | collective-permute-done | bytes 1056 | tf_op jit(solution)/shard_map/ppermute | solution.py:32
  50.6 1.2 collective-permute-done.11
  51.9 3.0 %collective-permute-start.12 = (f32[2,128]{1,0:T(2,128)S(1)}, f32[2,128]{1,0:T(2,128)S(1)}, u32[]{:S(2)}, u32[]{:S(2)}) collective-permute-start(f32[2,128]{1,0:T(2,128)S(1)} %fusion.28), channel_id=1, source_target_pairs={{0,8},{1,9},{2,10},{3,11},{4,12},{5,13},{6,14},{7,15},{8,0},{9,1},... | collective-permute-start | bytes 3080 | tf_op jit(solution)/shard_map/ppermute | solution.py:32
  55.2 1.3 collective-permute-done.12
  56.6 3.0 %collective-permute-start.13 = (f32[2,128]{1,0:T(2,128)S(1)}, f32[2,128]{1,0:T(2,128)S(1)}, u32[]{:S(2)}, u32[]{:S(2)}) collective-permute-start(f32[2,128]{1,0:T(2,128)S(1)} %fusion.20), channel_id=1, source_target_pairs={{0,16},{1,17},{2,18},{3,19},{4,20},{5,21},{6,22},{7,23},{8,24},{9,... | collective-permute-start | bytes 3080 | tf_op jit(solution)/shard_map/ppermute | solution.py:32
  59.6 1.7 %convolution_bitcast_fusion = f32[2,4,4,128]{3,0,2,1:T(2,128)S(1)} fusion(f32[2,4,4,128]{3,0,2,1:T(2,128)S(1)} %reshape.59, f32[4,4,128,128]{3,2,1,0:T(8,128)S(1)} %copy-done.2), kind=kOutput, calls=%fused_computation | convolution fusion | flops 6291456 | bytes 1081344 | tf_op jit(solution)/shard_map/xyij,sxyj->sxyi/dot_general | solution.py:60
  61.3 39.4 %all-reduce = (f32[2]{0:T(128)S(1)}, f32[2]{0:T(128)S(1)}) all-reduce(f32[2]{0:T(128)S(1)} %get-tuple-element.7, f32[2]{0:T(128)S(1)} %get-tuple-element.6), channel_id=1, replica_groups=mesh['gx'=8,'gy'=4] {'gx','gy'}, use_global_device_ids=true, to_apply=%region_1.0 | all-reduce | flops 4 | bytes 32 | tf_op jit(solution)/shard_map/psum | solution.py:119
  101.4 0.2 convolution_add_fusion.6
  101.8 0.2 convolution_add_fusion.5
  102.2 0.2 convolution_add_fusion.4
  102.5 0.2 convolution_add_fusion.3
  102.9 0.2 fusion.2
  103.1 1.1 multiply_reduce_fusion
  104.2 38.9 %psum.23 = f32[2]{0:T(128)S(1)} all-reduce(f32[2]{0:T(128)S(1)} %get-tuple-element.10), channel_id=1, replica_groups=mesh['gx'=8,'gy'=4] {'gx','gy'}, use_global_device_ids=true, to_apply=%region_5.0 | all-reduce | flops 2 | bytes 16 | tf_op jit(solution)/shard_map/psum | solution.py:126
  143.2 0.6 copy.18
  143.8 0.6 copy.19
  144.4 0.6 copy.20
  (61 shorter events, 5.2 us)
Async XLA Ops:
  0.6 1.2 copy-start
  0.6 2.5 %copy-start.4 = (f32[1,1,128,128]{3,2,1,0:T(8,128)S(1)}, f32[1,1,128,128]{3,2,1,0:T(8,128)}, u32[]{:S(2)}) copy-start(f32[1,1,128,128]{3,2,1,0:T(8,128)} %param.12) | copy-start | bytes 196612
  0.7 7.3 %copy-start.1 = (f32[1,1,4,128,128]{4,3,2,1,0:T(8,128)S(1)}, f32[1,1,4,128,128]{4,3,2,1,0:T(8,128)}, u32[]{:S(2)}) copy-start(f32[1,1,4,128,128]{4,3,2,1,0:T(8,128)} %param.13) | copy-start | bytes 786436
  0.7 19.2 %copy-start.2 = (f32[4,4,128,128]{3,2,1,0:T(8,128)S(1)}, f32[4,4,128,128]{3,2,1,0:T(8,128)}, u32[]{:S(2)}) copy-start(f32[4,4,128,128]{3,2,1,0:T(8,128)} %param.10) | copy-start | bytes 3145732
  3.4 4.6 %collective-permute-start = (f32[2,128]{1,0:T(2,128)S(1)}, f32[2,128]{1,0:T(2,128)S(1)}, u32[]{:S(2)}, u32[]{:S(2)}) collective-permute-start(f32[2,128]{1,0:T(2,128)S(1)} %fusion.56), channel_id=1, source_target_pairs={{0,1},{1,0},{2,3},{3,2},{4,5},{5,4},{6,7},{7,6},{8,9},{9,8},{10,11... | collective-permute-start | bytes 3080 | tf_op jit(solution)/shard_map/ppermute | solution.py:32
  8.1 4.6 %collective-permute-start.1 = (f32[2,128]{1,0:T(2,128)S(1)}, f32[2,128]{1,0:T(2,128)S(1)}, u32[]{:S(2)}, u32[]{:S(2)}) collective-permute-start(f32[2,128]{1,0:T(2,128)S(1)} %fusion.48), channel_id=1, source_target_pairs={{0,2},{1,3},{2,0},{3,1},{4,6},{5,7},{6,4},{7,5},{8,10},{9,11},{10,... | collective-permute-start | bytes 3080 | tf_op jit(solution)/shard_map/ppermute | solution.py:32
  12.9 1.2 collective-permute-start.2
  14.2 3.6 %collective-permute-start.3 = (f32[2,128]{1,0:T(2,128)S(1)}, f32[2,128]{1,0:T(2,128)S(1)}, u32[]{:S(2)}, u32[]{:S(2)}) collective-permute-start(f32[2,128]{1,0:T(2,128)S(1)} %fusion.32), channel_id=1, source_target_pairs={{0,8},{1,9},{2,10},{3,11},{4,12},{5,13},{6,14},{7,15},{8,0},{9,1},... | collective-permute-start | bytes 3080 | tf_op jit(solution)/shard_map/ppermute | solution.py:32
  18.0 3.9 %collective-permute-start.4 = (f32[2,128]{1,0:T(2,128)S(1)}, f32[2,128]{1,0:T(2,128)S(1)}, u32[]{:S(2)}, u32[]{:S(2)}) collective-permute-start(f32[2,128]{1,0:T(2,128)S(1)} %fusion.24), channel_id=1, source_target_pairs={{0,16},{1,17},{2,18},{3,19},{4,20},{5,21},{6,22},{7,23},{8,24},{9,... | collective-permute-start | bytes 3080 | tf_op jit(solution)/shard_map/ppermute | solution.py:32
  19.9 2.0 %copy-start.3 = (f32[1,1,5,128,128]{4,3,2,1,0:T(8,128)S(1)}, f32[1,1,5,128,128]{4,3,2,1,0:T(8,128)}, u32[]{:S(2)}) copy-start(f32[1,1,5,128,128]{4,3,2,1,0:T(8,128)} %param.15) | copy-start | bytes 983044
  23.4 0.9 copy-start.6
  24.4 1.0 copy-start.7
  25.4 4.3 %collective-permute-start.6 = (f32[3,1,128]{2,0,1:T(4,128)S(1)}, f32[3,1,128]{2,0,1:T(4,128)S(1)}, u32[]{:S(2)}, u32[]{:S(2)}) collective-permute-start(f32[3,1,128]{2,0,1:T(4,128)S(1)} %get-tuple-element.20), channel_id=1, source_target_pairs={{4,0},{8,4},{12,8},{16,12},{20,16},{24,20},{28,24},{5,1},{9,5},{13... | collective-permute-start | bytes 4616 | tf_op jit(solution)/shard_map/ppermute | solution.py:22
  26.7 3.8 %collective-permute-start.5 = (f32[3,1,128]{2,0,1:T(4,128)S(1)}, f32[3,1,128]{2,0,1:T(4,128)S(1)}, u32[]{:S(2)}, u32[]{:S(2)}) collective-permute-start(f32[3,1,128]{2,0,1:T(4,128)S(1)} %get-tuple-element.19), channel_id=1, source_target_pairs={{0,4},{4,8},{8,12},{12,16},{16,20},{20,24},{24,28},{1,5},{5,9},{9,... | collective-permute-start | bytes 4616 | tf_op jit(solution)/shard_map/ppermute | solution.py:20
  30.7 5.3 %collective-permute-start.7 = (f32[3,18,1]{2,0,1:T(4,128)S(1)}, f32[3,18,1]{2,0,1:T(4,128)S(1)}, u32[]{:S(2)}, u32[]{:S(2)}) collective-permute-start(f32[3,18,1]{2,0,1:T(4,128)S(1)} %get-tuple-element.14), channel_id=1, source_target_pairs={{0,1},{1,2},{2,3},{4,5},{5,6},{6,7},{8,9},{9,10},{10,11},{12,13},{... | collective-permute-start | bytes 656 | tf_op jit(solution)/shard_map/ppermute | solution.py:20
  34.2 6.0 %collective-permute-start.8 = (f32[3,18,1]{2,0,1:T(4,128)S(1)}, f32[3,18,1]{2,0,1:T(4,128)S(1)}, u32[]{:S(2)}, u32[]{:S(2)}) collective-permute-start(f32[3,18,1]{2,0,1:T(4,128)S(1)} %get-tuple-element.13), channel_id=1, source_target_pairs={{1,0},{2,1},{3,2},{5,4},{6,5},{7,6},{9,8},{10,9},{11,10},{13,12},{... | collective-permute-start | bytes 656 | tf_op jit(solution)/shard_map/ppermute | solution.py:22
  40.4 0.7 copy-start.5
  42.2 3.6 %collective-permute-start.9 = (f32[2,128]{1,0:T(2,128)S(1)}, f32[2,128]{1,0:T(2,128)S(1)}, u32[]{:S(2)}, u32[]{:S(2)}) collective-permute-start(f32[2,128]{1,0:T(2,128)S(1)} %fusion.52), channel_id=1, source_target_pairs={{0,1},{1,0},{2,3},{3,2},{4,5},{5,4},{6,7},{7,6},{8,9},{9,8},{10,11... | collective-permute-start | bytes 3080 | tf_op jit(solution)/shard_map/ppermute | solution.py:32
  45.9 4.5 %collective-permute-start.10 = (f32[2,128]{1,0:T(2,128)S(1)}, f32[2,128]{1,0:T(2,128)S(1)}, u32[]{:S(2)}, u32[]{:S(2)}) collective-permute-start(f32[2,128]{1,0:T(2,128)S(1)} %fusion.44), channel_id=1, source_target_pairs={{0,2},{1,3},{2,0},{3,1},{4,6},{5,7},{6,4},{7,5},{8,10},{9,11},{10,... | collective-permute-start | bytes 3080 | tf_op jit(solution)/shard_map/ppermute | solution.py:32
  50.6 1.2 collective-permute-start.11
  51.9 4.6 %collective-permute-start.12 = (f32[2,128]{1,0:T(2,128)S(1)}, f32[2,128]{1,0:T(2,128)S(1)}, u32[]{:S(2)}, u32[]{:S(2)}) collective-permute-start(f32[2,128]{1,0:T(2,128)S(1)} %fusion.28), channel_id=1, source_target_pairs={{0,8},{1,9},{2,10},{3,11},{4,12},{5,13},{6,14},{7,15},{8,0},{9,1},... | collective-permute-start | bytes 3080 | tf_op jit(solution)/shard_map/ppermute | solution.py:32
  56.6 44.4 %collective-permute-start.13 = (f32[2,128]{1,0:T(2,128)S(1)}, f32[2,128]{1,0:T(2,128)S(1)}, u32[]{:S(2)}, u32[]{:S(2)}) collective-permute-start(f32[2,128]{1,0:T(2,128)S(1)} %fusion.20), channel_id=1, source_target_pairs={{0,16},{1,17},{2,18},{3,19},{4,20},{5,21},{6,22},{7,23},{8,24},{9,... | collective-permute-start | bytes 3080 | tf_op jit(solution)/shard_map/ppermute | solution.py:32
where the time goes:
time: 146 us; the launch traced here: 145 us
  blocking collectives  78.3 us (54%)
  starting transfers between devices  29.2 us (20%)
  waiting for transfers between devices  17 us (12%)
  matrix products  13.2 us (9%)
  local copies, waits for them, and re-layouts  5.87 us (4%)
    psum x1, blocking collectives, on_device(): rz_old = lax.psum(local_rz, ('gx', 'gy'))  39.4 us
    psum x1, blocking collectives, on_device(): rz_new = lax.psum(jnp.sum(residual * second_z, axis=(1, 2)), ('gx', 'gy'))  38.9 us
    ppermute x10, starting transfers between devices, from_partner(): return lax.ppermute(value, axis, pairs)  20.1 us
    ppermute x10, waiting for transfers between devices, from_partner(): return lax.ppermute(value, axis, pairs)  11.5 us
    ppermute x2, starting transfers between devices, extended(): lax.ppermute(tail, axis, [(i, (i + 1) % count) for i in range(ends)])  6.55 us
    ppermute x2, waiting for transfers between devices, extended(): lax.ppermute(head, axis, [((i + 1) % count, i) for i in range(ends)])  4.23 us
    unnamed x20, local copies, waits for them, and re-layouts  4.17 us
    dot_general x2, matrix products, leaf_apply(): jnp.einsum('xyij,sxyj->sxyi', leaf_inverse, grouped, precision=HIGHEST)  3.46 us
  transfers between devices with their start and end apart: 14, of which 11 were waited for; matrix products, arithmetic and copies ran while one was open for 4% of the time, Pallas kernels for 0%

commit v1 on v0

--- a/solution.py
+++ b/solution.py
@@ -116,7 +116,9 @@
     )
     first_z = apply_inverse(right_side)
     local_rz = jnp.sum(right_side * first_z, axis=(1, 2))
-    rz_old = lax.psum(local_rz, ("gx", "gy"))
+    rz_old = local_rz
+    for mesh_axis in ("gy", "gx"):
+        rz_old = lax.psum(rz_old, mesh_axis)
     applied = stencil(first_z, conductivity)
     curvature = lax.psum(jnp.sum(first_z * applied, axis=(1, 2)), ("gx", "gy"))
     step_size = (rz_old / curvature)[:, None, None]

time: 146 us -> 168 us (1.15)
  blocking collectives: 78.3 us -> 100 us
    psum x1 -> x3, blocking collectives: 39.4 us -> 60.9 us  [the longest x1 37.8 us: on_device(): curvature = lax.psum(jnp.sum(first_z * applied, axis=(1, 2)), ('gx', 'gy'))]
  transfers between devices with their start and end apart: 14 -> 14, of which waited for: 11 -> 11; matrix products, arithmetic and copies ran while one was open for 4% -> 3% of each run, Pallas kernels for 0% -> 0%
where the time goes in v1:
time: 168 us; the launch traced here: 167 us
  blocking collectives  100 us (60%)
  starting transfers between devices  29.2 us (17%)
  waiting for transfers between devices  17 us (10%)
  matrix products  13.2 us (8%)
  local copies, waits for them, and re-layouts  5.87 us (3%)
    psum x1, blocking collectives, on_device(): rz_new = lax.psum(jnp.sum(residual * second_z, axis=(1, 2)), ('gx', 'gy'))  39.5 us
    psum x1, blocking collectives, on_device(): curvature = lax.psum(jnp.sum(first_z * applied, axis=(1, 2)), ('gx', 'gy'))  37.8 us
    psum x2, blocking collectives, on_device(): rz_old = lax.psum(rz_old, mesh_axis)  23 us
    ppermute x10, starting transfers between devices, from_partner(): return lax.ppermute(value, axis, pairs)  20.1 us
    ppermute x10, waiting for transfers between devices, from_partner(): return lax.ppermute(value, axis, pairs)  11.5 us
    ppermute x2, starting transfers between devices, extended(): lax.ppermute(tail, axis, [(i, (i + 1) % count) for i in range(ends)])  6.55 us
    ppermute x2, waiting for transfers between devices, extended(): lax.ppermute(head, axis, [((i + 1) % count, i) for i in range(ends)])  4.23 us
    unnamed x20, local copies, waits for them, and re-layouts  4.17 us
  transfers between devices with their start and end apart: 14, of which 11 were waited for; matrix products, arithmetic and copies ran while one was open for 3% of the time, Pallas kernels for 0%

profile of v1, /device:TPU:0, one launch (start us, length us, event | category | flops | bytes accessed | tf_op | source)
XLA Modules:
  0.0 167.2 jit_solution(12495824912442685644)
XLA Ops:
  0.7 1.2 copy-done
  1.9 1.3 convolution_bitcast_fusion.3
  3.4 3.1 %collective-permute-start = (f32[2,128]{1,0:T(2,128)S(1)}, f32[2,128]{1,0:T(2,128)S(1)}, u32[]{:S(2)}, u32[]{:S(2)}) collective-permute-start(f32[2,128]{1,0:T(2,128)S(1)} %fusion.56), channel_id=1, source_target_pairs={{0,1},{1,0},{2,3},{3,2},{4,5},{5,4},{6,7},{7,6},{8,9},{9,8},{10,11... | collective-permute-start | bytes 3080 | tf_op jit(solution)/shard_map/ppermute | solution.py:32
  6.4 1.6 collective-permute-done
  8.1 3.1 %collective-permute-start.1 = (f32[2,128]{1,0:T(2,128)S(1)}, f32[2,128]{1,0:T(2,128)S(1)}, u32[]{:S(2)}, u32[]{:S(2)}) collective-permute-start(f32[2,128]{1,0:T(2,128)S(1)} %fusion.48), channel_id=1, source_target_pairs={{0,2},{1,3},{2,0},{3,1},{4,6},{5,7},{6,4},{7,5},{8,10},{9,11},{10,... | collective-permute-start | bytes 3080 | tf_op jit(solution)/shard_map/ppermute | solution.py:32
  11.2 1.6 collective-permute-done.1
  12.9 1.2 collective-permute-done.2
  14.2 1.8 %collective-permute-start.3 = (f32[2,128]{1,0:T(2,128)S(1)}, f32[2,128]{1,0:T(2,128)S(1)}, u32[]{:S(2)}, u32[]{:S(2)}) collective-permute-start(f32[2,128]{1,0:T(2,128)S(1)} %fusion.32), channel_id=1, source_target_pairs={{0,8},{1,9},{2,10},{3,11},{4,12},{5,13},{6,14},{7,15},{8,0},{9,1},... | collective-permute-start | bytes 3080 | tf_op jit(solution)/shard_map/ppermute | solution.py:32
  16.1 0.8 reshape.54
  17.0 0.8 collective-permute-done.3
  18.0 1.9 %collective-permute-start.4 = (f32[2,128]{1,0:T(2,128)S(1)}, f32[2,128]{1,0:T(2,128)S(1)}, u32[]{:S(2)}, u32[]{:S(2)}) collective-permute-start(f32[2,128]{1,0:T(2,128)S(1)} %fusion.24), channel_id=1, source_target_pairs={{0,16},{1,17},{2,18},{3,19},{4,20},{5,21},{6,22},{7,23},{8,24},{9,... | collective-permute-start | bytes 3080 | tf_op jit(solution)/shard_map/ppermute | solution.py:32
  19.9 1.7 %convolution_bitcast_fusion.1 = f32[2,4,4,128]{3,0,2,1:T(2,128)S(1)} fusion(f32[2,4,4,128]{3,0,2,1:T(2,128)S(1)} %reshape.55, f32[4,4,128,128]{3,2,1,0:T(8,128)S(1)} %copy-done.2), kind=kOutput, calls=%fused_computation.1 | convolution fusion | flops 6291456 | bytes 1081344 | tf_op jit(solution)/shard_map/xyij,sxyj->sxyi/dot_general | solution.py:60
  22.2 0.2 convolution_add_fusion.11
  22.6 0.2 convolution_add_fusion.10
  23.0 0.2 convolution_add_fusion.9
  23.4 0.2 convolution_add_fusion.8
  23.8 0.5 copy-done.6
  24.4 1.0 convolution_add_fusion.1
  25.4 1.3 collective-permute-start.6
  26.7 3.0 %collective-permute-start.5 = (f32[3,1,128]{2,0,1:T(4,128)S(1)}, f32[3,1,128]{2,0,1:T(4,128)S(1)}, u32[]{:S(2)}, u32[]{:S(2)}) collective-permute-start(f32[3,1,128]{2,0,1:T(4,128)S(1)} %get-tuple-element.17), channel_id=1, source_target_pairs={{0,4},{4,8},{8,12},{12,16},{16,20},{20,24},{24,28},{1,5},{5,9},{9,... | collective-permute-start | bytes 4616 | tf_op jit(solution)/shard_map/ppermute | solution.py:20
  29.8 0.8 collective-permute-done.5
  30.7 3.5 %collective-permute-start.7 = (f32[3,18,1]{2,0,1:T(4,128)S(1)}, f32[3,18,1]{2,0,1:T(4,128)S(1)}, u32[]{:S(2)}, u32[]{:S(2)}) collective-permute-start(f32[3,18,1]{2,0,1:T(4,128)S(1)} %get-tuple-element.12), channel_id=1, source_target_pairs={{0,1},{1,2},{2,3},{4,5},{5,6},{6,7},{8,9},{9,10},{10,11},{12,13},{... | collective-permute-start | bytes 656 | tf_op jit(solution)/shard_map/ppermute | solution.py:20
  34.2 1.3 collective-permute-start.8
  35.5 0.5 collective-permute-done.7
  36.0 4.2 %collective-permute-done.8 = f32[3,18,1]{2,0,1:T(4,128)S(1)} collective-permute-done((f32[3,18,1]{2,0,1:T(4,128)S(1)}, f32[3,18,1]{2,0,1:T(4,128)S(1)}, u32[]{:S(2)}, u32[]{:S(2)}) %collective-permute-start.8) | collective-permute-done | bytes 248 | tf_op jit(solution)/shard_map/ppermute | solution.py:22
  40.5 0.6 copy-done.5
  41.1 0.3 multiply_reduce_fusion.1
  41.4 0.6 convolution_bitcast_fusion.2
  42.2 1.6 collective-permute-start.9
  43.8 2.0 %collective-permute-done.9 = f32[2,128]{1,0:T(2,128)S(1)} collective-permute-done((f32[2,128]{1,0:T(2,128)S(1)}, f32[2,128]{1,0:T(2,128)S(1)}, u32[]{:S(2)}, u32[]{:S(2)}) %collective-permute-start.9) | collective-permute-done | bytes 1056 | tf_op jit(solution)/shard_map/ppermute | solution.py:32
  45.9 2.6 %collective-permute-start.10 = (f32[2,128]{1,0:T(2,128)S(1)}, f32[2,128]{1,0:T(2,128)S(1)}, u32[]{:S(2)}, u32[]{:S(2)}) collective-permute-start(f32[2,128]{1,0:T(2,128)S(1)} %fusion.44), channel_id=1, source_target_pairs={{0,2},{1,3},{2,0},{3,1},{4,6},{5,7},{6,4},{7,5},{8,10},{9,11},{10,... | collective-permute-start | bytes 3080 | tf_op jit(solution)/shard_map/ppermute | solution.py:32
  48.5 1.9 %collective-permute-done.10 = f32[2,128]{1,0:T(2,128)S(1)} collective-permute-done((f32[2,128]{1,0:T(2,128)S(1)}, f32[2,128]{1,0:T(2,128)S(1)}, u32[]{:S(2)}, u32[]{:S(2)}) %collective-permute-start.10) | collective-permute-done | bytes 1056 | tf_op jit(solution)/shard_map/ppermute | solution.py:32
  50.6 1.2 collective-permute-done.11
  51.9 3.0 %collective-permute-start.12 = (f32[2,128]{1,0:T(2,128)S(1)}, f32[2,128]{1,0:T(2,128)S(1)}, u32[]{:S(2)}, u32[]{:S(2)}) collective-permute-start(f32[2,128]{1,0:T(2,128)S(1)} %fusion.28), channel_id=1, source_target_pairs={{0,8},{1,9},{2,10},{3,11},{4,12},{5,13},{6,14},{7,15},{8,0},{9,1},... | collective-permute-start | bytes 3080 | tf_op jit(solution)/shard_map/ppermute | solution.py:32
  55.2 1.3 collective-permute-done.12
  56.6 3.0 %collective-permute-start.13 = (f32[2,128]{1,0:T(2,128)S(1)}, f32[2,128]{1,0:T(2,128)S(1)}, u32[]{:S(2)}, u32[]{:S(2)}) collective-permute-start(f32[2,128]{1,0:T(2,128)S(1)} %fusion.20), channel_id=1, source_target_pairs={{0,16},{1,17},{2,18},{3,19},{4,20},{5,21},{6,22},{7,23},{8,24},{9,... | collective-permute-start | bytes 3080 | tf_op jit(solution)/shard_map/ppermute | solution.py:32
  59.6 1.7 %convolution_bitcast_fusion = f32[2,4,4,128]{3,0,2,1:T(2,128)S(1)} fusion(f32[2,4,4,128]{3,0,2,1:T(2,128)S(1)} %reshape.59, f32[4,4,128,128]{3,2,1,0:T(8,128)S(1)} %copy-done.2), kind=kOutput, calls=%fused_computation | convolution fusion | flops 6291456 | bytes 1081344 | tf_op jit(solution)/shard_map/xyij,sxyj->sxyi/dot_general | solution.py:60
  61.3 10.4 %psum.28 = f32[2]{0:T(128)S(1)} all-reduce(f32[2]{0:T(128)S(1)} %get-tuple-element.7), channel_id=1, replica_groups=mesh['gx'=8,'gy'=4] {'gy'}, use_global_device_ids=true, to_apply=%region_1.0 | all-reduce | flops 2 | bytes 16 | tf_op jit(solution)/shard_map/psum | solution.py:121
  71.7 37.8 %psum.30 = f32[2]{0:T(128)S(1)} all-reduce(f32[2]{0:T(128)S(1)} %get-tuple-element.6), channel_id=1, replica_groups=mesh['gx'=8,'gy'=4] {'gx','gy'}, use_global_device_ids=true, to_apply=%region_4.0 | all-reduce | flops 2 | bytes 16 | tf_op jit(solution)/shard_map/psum | solution.py:123
  109.6 12.7 %psum.29 = f32[2]{0:T(128)S(1)} all-reduce(f32[2]{0:T(128)S(1)} %psum.28), channel_id=1, replica_groups=mesh['gx'=8,'gy'=4] {'gx'}, use_global_device_ids=true, to_apply=%region_2.0 | all-reduce | flops 2 | bytes 16 | tf_op jit(solution)/shard_map/psum | solution.py:121
  123.2 0.2 convolution_add_fusion.5
  123.6 0.2 convolution_add_fusion.4
  124.0 0.2 convolution_add_fusion.3
  124.6 1.1 multiply_reduce_fusion
  125.7 39.5 %psum.31 = f32[2]{0:T(128)S(1)} all-reduce(f32[2]{0:T(128)S(1)} %get-tuple-element.8), channel_id=1, replica_groups=mesh['gx'=8,'gy'=4] {'gx','gy'}, use_global_device_ids=true, to_apply=%region_6.0 | all-reduce | flops 2 | bytes 16 | tf_op jit(solution)/shard_map/psum | solution.py:128
  165.3 0.6 copy.18
  166.0 0.6 copy.19
  166.6 0.6 copy.20
  (63 shorter events, 5.6 us)
Async XLA Ops:
  0.6 1.2 copy-start
  0.6 2.5 %copy-start.4 = (f32[1,1,128,128]{3,2,1,0:T(8,128)S(1)}, f32[1,1,128,128]{3,2,1,0:T(8,128)}, u32[]{:S(2)}) copy-start(f32[1,1,128,128]{3,2,1,0:T(8,128)} %param.12) | copy-start | bytes 196612
  0.7 7.3 %copy-start.1 = (f32[1,1,4,128,128]{4,3,2,1,0:T(8,128)S(1)}, f32[1,1,4,128,128]{4,3,2,1,0:T(8,128)}, u32[]{:S(2)}) copy-start(f32[1,1,4,128,128]{4,3,2,1,0:T(8,128)} %param.13) | copy-start | bytes 786436
  0.7 19.2 %copy-start.2 = (f32[4,4,128,128]{3,2,1,0:T(8,128)S(1)}, f32[4,4,128,128]{3,2,1,0:T(8,128)}, u32[]{:S(2)}) copy-start(f32[4,4,128,128]{3,2,1,0:T(8,128)} %param.10) | copy-start | bytes 3145732
  3.4 4.6 %collective-permute-start = (f32[2,128]{1,0:T(2,128)S(1)}, f32[2,128]{1,0:T(2,128)S(1)}, u32[]{:S(2)}, u32[]{:S(2)}) collective-permute-start(f32[2,128]{1,0:T(2,128)S(1)} %fusion.56), channel_id=1, source_target_pairs={{0,1},{1,0},{2,3},{3,2},{4,5},{5,4},{6,7},{7,6},{8,9},{9,8},{10,11... | collective-permute-start | bytes 3080 | tf_op jit(solution)/shard_map/ppermute | solution.py:32
  8.1 4.6 %collective-permute-start.1 = (f32[2,128]{1,0:T(2,128)S(1)}, f32[2,128]{1,0:T(2,128)S(1)}, u32[]{:S(2)}, u32[]{:S(2)}) collective-permute-start(f32[2,128]{1,0:T(2,128)S(1)} %fusion.48), channel_id=1, source_target_pairs={{0,2},{1,3},{2,0},{3,1},{4,6},{5,7},{6,4},{7,5},{8,10},{9,11},{10,... | collective-permute-start | bytes 3080 | tf_op jit(solution)/shard_map/ppermute | solution.py:32
  12.9 1.2 collective-permute-start.2
  14.2 3.6 %collective-permute-start.3 = (f32[2,128]{1,0:T(2,128)S(1)}, f32[2,128]{1,0:T(2,128)S(1)}, u32[]{:S(2)}, u32[]{:S(2)}) collective-permute-start(f32[2,128]{1,0:T(2,128)S(1)} %fusion.32), channel_id=1, source_target_pairs={{0,8},{1,9},{2,10},{3,11},{4,12},{5,13},{6,14},{7,15},{8,0},{9,1},... | collective-permute-start | bytes 3080 | tf_op jit(solution)/shard_map/ppermute | solution.py:32
  18.0 3.9 %collective-permute-start.4 = (f32[2,128]{1,0:T(2,128)S(1)}, f32[2,128]{1,0:T(2,128)S(1)}, u32[]{:S(2)}, u32[]{:S(2)}) collective-permute-start(f32[2,128]{1,0:T(2,128)S(1)} %fusion.24), channel_id=1, source_target_pairs={{0,16},{1,17},{2,18},{3,19},{4,20},{5,21},{6,22},{7,23},{8,24},{9,... | collective-permute-start | bytes 3080 | tf_op jit(solution)/shard_map/ppermute | solution.py:32
  19.9 2.0 %copy-start.3 = (f32[1,1,5,128,128]{4,3,2,1,0:T(8,128)S(1)}, f32[1,1,5,128,128]{4,3,2,1,0:T(8,128)}, u32[]{:S(2)}) copy-start(f32[1,1,5,128,128]{4,3,2,1,0:T(8,128)} %param.15) | copy-start | bytes 983044
  23.4 0.9 copy-start.6
  24.4 1.0 copy-start.7
  25.4 4.3 %collective-permute-start.6 = (f32[3,1,128]{2,0,1:T(4,128)S(1)}, f32[3,1,128]{2,0,1:T(4,128)S(1)}, u32[]{:S(2)}, u32[]{:S(2)}) collective-permute-start(f32[3,1,128]{2,0,1:T(4,128)S(1)} %get-tuple-element.18), channel_id=1, source_target_pairs={{4,0},{8,4},{12,8},{16,12},{20,16},{24,20},{28,24},{5,1},{9,5},{13... | collective-permute-start | bytes 4616 | tf_op jit(solution)/shard_map/ppermute | solution.py:22
  26.7 3.8 %collective-permute-start.5 = (f32[3,1,128]{2,0,1:T(4,128)S(1)}, f32[3,1,128]{2,0,1:T(4,128)S(1)}, u32[]{:S(2)}, u32[]{:S(2)}) collective-permute-start(f32[3,1,128]{2,0,1:T(4,128)S(1)} %get-tuple-element.17), channel_id=1, source_target_pairs={{0,4},{4,8},{8,12},{12,16},{16,20},{20,24},{24,28},{1,5},{5,9},{9,... | collective-permute-start | bytes 4616 | tf_op jit(solution)/shard_map/ppermute | solution.py:20
  30.7 5.3 %collective-permute-start.7 = (f32[3,18,1]{2,0,1:T(4,128)S(1)}, f32[3,18,1]{2,0,1:T(4,128)S(1)}, u32[]{:S(2)}, u32[]{:S(2)}) collective-permute-start(f32[3,18,1]{2,0,1:T(4,128)S(1)} %get-tuple-element.12), channel_id=1, source_target_pairs={{0,1},{1,2},{2,3},{4,5},{5,6},{6,7},{8,9},{9,10},{10,11},{12,13},{... | collective-permute-start | bytes 656 | tf_op jit(solution)/shard_map/ppermute | solution.py:20
  34.2 6.0 %collective-permute-start.8 = (f32[3,18,1]{2,0,1:T(4,128)S(1)}, f32[3,18,1]{2,0,1:T(4,128)S(1)}, u32[]{:S(2)}, u32[]{:S(2)}) collective-permute-start(f32[3,18,1]{2,0,1:T(4,128)S(1)} %get-tuple-element.11), channel_id=1, source_target_pairs={{1,0},{2,1},{3,2},{5,4},{6,5},{7,6},{9,8},{10,9},{11,10},{13,12},{... | collective-permute-start | bytes 656 | tf_op jit(solution)/shard_map/ppermute | solution.py:22
  40.4 0.7 copy-start.5
  42.2 3.6 %collective-permute-start.9 = (f32[2,128]{1,0:T(2,128)S(1)}, f32[2,128]{1,0:T(2,128)S(1)}, u32[]{:S(2)}, u32[]{:S(2)}) collective-permute-start(f32[2,128]{1,0:T(2,128)S(1)} %fusion.52), channel_id=1, source_target_pairs={{0,1},{1,0},{2,3},{3,2},{4,5},{5,4},{6,7},{7,6},{8,9},{9,8},{10,11... | collective-permute-start | bytes 3080 | tf_op jit(solution)/shard_map/ppermute | solution.py:32
  45.9 4.5 %collective-permute-start.10 = (f32[2,128]{1,0:T(2,128)S(1)}, f32[2,128]{1,0:T(2,128)S(1)}, u32[]{:S(2)}, u32[]{:S(2)}) collective-permute-start(f32[2,128]{1,0:T(2,128)S(1)} %fusion.44), channel_id=1, source_target_pairs={{0,2},{1,3},{2,0},{3,1},{4,6},{5,7},{6,4},{7,5},{8,10},{9,11},{10,... | collective-permute-start | bytes 3080 | tf_op jit(solution)/shard_map/ppermute | solution.py:32
  50.6 1.2 collective-permute-start.11
  51.9 4.6 %collective-permute-start.12 = (f32[2,128]{1,0:T(2,128)S(1)}, f32[2,128]{1,0:T(2,128)S(1)}, u32[]{:S(2)}, u32[]{:S(2)}) collective-permute-start(f32[2,128]{1,0:T(2,128)S(1)} %fusion.28), channel_id=1, source_target_pairs={{0,8},{1,9},{2,10},{3,11},{4,12},{5,13},{6,14},{7,15},{8,0},{9,1},... | collective-permute-start | bytes 3080 | tf_op jit(solution)/shard_map/ppermute | solution.py:32
  56.6 65.8 %collective-permute-start.13 = (f32[2,128]{1,0:T(2,128)S(1)}, f32[2,128]{1,0:T(2,128)S(1)}, u32[]{:S(2)}, u32[]{:S(2)}) collective-permute-start(f32[2,128]{1,0:T(2,128)S(1)} %fusion.20), channel_id=1, source_target_pairs={{0,16},{1,17},{2,18},{3,19},{4,20},{5,21},{6,22},{7,23},{8,24},{9,... | collective-permute-start | bytes 3080 | tf_op jit(solution)/shard_map/ppermute | solution.py:32
